TPU v7x, 32 devices: a whole 2x2x4 slice. The times are simulated.
32 devices in a mesh: ctx: 16 (over z, x, core), fsdp: 2 (over y).
Axes of the slice: x: 2, y: 2, z: 4, core: 2. Of those that a mesh axis runs over, the one named last changes fastest.
Arguments:
- tokens: bfloat16 [2, 4096, 768], P('fsdp', 'ctx'), may hold values from -6 to 6
- query_weight: bfloat16 [768, 768], P('fsdp'), may hold values from -0.21875 to 0.21875
- query_bias: bfloat16 [768], P('fsdp'), may hold values from -1.5 to 1.5
- key_weight: bfloat16 [768, 768], P('fsdp'), may hold values from -0.21875 to 0.21875
- value_weight: bfloat16 [768, 768], P('fsdp'), may hold values from -0.21875 to 0.21875
- value_bias: bfloat16 [768], P('fsdp'), may hold values from -1.5 to 1.5
- out_weight: bfloat16 [768, 768], P('fsdp'), may hold values from -1.25 to 1.25
- out_bias: bfloat16 [768], P('fsdp'), may hold values from -1.5 to 1.5
- first_gain: bfloat16 [768], P('fsdp'), may hold values from 0.5 to 1.5
- first_shift: bfloat16 [768], P('fsdp'), may hold values from -1.5 to 1.5
- inner_weight: bfloat16 [768, 3072], P('fsdp'), may hold values from -0.21875 to 0.21875
- inner_bias: bfloat16 [3072], P('fsdp'), may hold values from -1.5 to 1.5
- outer_weight: bfloat16 [3072, 768], P('fsdp'), may hold values from -0.109375 to 0.109375
- outer_bias: bfloat16 [768], P('fsdp'), may hold values from -1.5 to 1.5
- second_gain: bfloat16 [768], P('fsdp'), may hold values from 0.5 to 1.5
- second_shift: bfloat16 [768], P('fsdp'), may hold values from -1.5 to 1.5
- doc_lengths: int32 [2, 48], P('fsdp'), may hold values from 1 to 2304, 4096 in all within a row
- grad_output: bfloat16 [2, 4096, 768], P('fsdp', 'ctx'), may hold values from -6 to 6
Outputs:
- output: bfloat16 [2, 4096, 768], P('fsdp', 'ctx')
- grad_tokens: float32 [2, 4096, 768], P('fsdp', 'ctx')
- grad_query_weight: float32 [768, 768], P('fsdp')
- grad_query_bias: float32 [768], P('fsdp')
- grad_key_weight: float32 [768, 768], P('fsdp')
- grad_value_weight: float32 [768, 768], P('fsdp')
- grad_value_bias: float32 [768], P('fsdp')
- grad_out_weight: float32 [768, 768], P('fsdp')
- grad_out_bias: float32 [768], P('fsdp')
- grad_first_gain: float32 [768], P('fsdp')
- grad_first_shift: float32 [768], P('fsdp')
- grad_inner_weight: float32 [768, 3072], P('fsdp')
- grad_inner_bias: float32 [3072], P('fsdp')
- grad_outer_weight: float32 [3072, 768], P('fsdp')
- grad_outer_bias: float32 [768], P('fsdp')
- grad_second_gain: float32 [768], P('fsdp')
- grad_second_shift: float32 [768], P('fsdp')
Inputs may be any that keep to these rules, and one draw needn't show every extreme that they name: `doc_lengths`: each row holds the 48 document lengths of one sequence in order; they sum to 4096 and the longest is exactly 2304.
All inputs are finite; a program needn't handle non-finite values.
Results may differ from a plain program's by a relative error of at most 0.018.
Values may be sent and summed in bfloat16 or wider, within the bound.
No kernel may reach another device: no remote copies, remote signals or barrier semaphores. Data moves between devices by JAX's collectives and lax.ppermute only.
A program may use at most 384 MiB of HBM per device.

v0:
```python
import math
import jax
import jax.numpy as jnp
from jax import lax
from jax.sharding import PartitionSpec as P

H = 12
HD = 64
eps = 1e-12


def layer_norm(r, gain, shift):
    mean = jnp.mean(r, axis=-1, keepdims=True)
    centered = r - mean
    var = jnp.mean(centered * centered, axis=-1, keepdims=True)
    return centered * lax.rsqrt(var + eps) * gain + shift


def gelu_exact(v):
    return jax.nn.gelu(v, approximate=False)


def inner_rows(left, right):
    return lax.dot_general(
        left, right, (((1,), (1,)), ((), ())), preferred_element_type=jnp.float32
    )


def inner_cols(left, right):
    return lax.dot_general(
        left, right, (((0,), (0,)), ((), ())), preferred_element_type=jnp.float32
    )


def segment_of(places, lengths):
    ends = jnp.cumsum(lengths)
    return jnp.sum((places[:, None] >= ends[None, :]).astype(jnp.int32), axis=1)


def masked_scores(query_part, key_part, allowed, scale):
    raw = inner_rows(query_part, key_part) * scale
    return jnp.where(allowed, raw, jnp.float32(-1e30))


def on_device(
    tokens,
    query_weight,
    query_bias,
    key_weight,
    value_weight,
    value_bias,
    out_weight,
    out_bias,
    first_gain,
    first_shift,
    inner_weight,
    inner_bias,
    outer_weight,
    outer_bias,
    second_gain,
    second_shift,
    doc_lengths,
    grad_output,
):
    rows = tokens.shape[1]
    width = tokens.shape[2]
    scale = 1.0 / math.sqrt(HD)
    length_total = rows * lax.axis_size("ctx")
    gathered = (
        lax.all_gather(query_weight, "fsdp", axis=0, tiled=True),
        lax.all_gather(query_bias, "fsdp", axis=0, tiled=True),
        lax.all_gather(key_weight, "fsdp", axis=0, tiled=True),
        lax.all_gather(value_weight, "fsdp", axis=0, tiled=True),
        lax.all_gather(value_bias, "fsdp", axis=0, tiled=True),
        lax.all_gather(out_weight, "fsdp", axis=0, tiled=True),
        lax.all_gather(out_bias, "fsdp", axis=0, tiled=True),
        lax.all_gather(first_gain, "fsdp", axis=0, tiled=True),
        lax.all_gather(first_shift, "fsdp", axis=0, tiled=True),
        lax.all_gather(inner_weight, "fsdp", axis=0, tiled=True),
        lax.all_gather(inner_bias, "fsdp", axis=0, tiled=True),
        lax.all_gather(outer_weight, "fsdp", axis=0, tiled=True),
        lax.all_gather(outer_bias, "fsdp", axis=0, tiled=True),
        lax.all_gather(second_gain, "fsdp", axis=0, tiled=True),
        lax.all_gather(second_shift, "fsdp", axis=0, tiled=True),
    )
    (
        query_full,
        qbias_full,
        key_full,
        value_full,
        vbias_full,
        out_full,
        obias_full,
        gain_one,
        shift_one,
        inner_full,
        ibias_full,
        outer_full,
        outbias_full,
        gain_two,
        shift_two,
    ) = gathered
    local_in = tokens[0]
    local_float = local_in.astype(jnp.float32)
    query_low = (
        jnp.dot(local_in, query_full, preferred_element_type=jnp.float32)
        + qbias_full.astype(jnp.float32)
    ).astype(jnp.bfloat16)
    key_low = jnp.dot(local_in, key_full, preferred_element_type=jnp.float32).astype(jnp.bfloat16)
    value_low = (
        jnp.dot(local_in, value_full, preferred_element_type=jnp.float32)
        + vbias_full.astype(jnp.float32)
    ).astype(jnp.bfloat16)
    first_row = lax.axis_index("ctx") * rows
    places_own = first_row + jnp.arange(rows, dtype=jnp.int32)
    segs_own = segment_of(places_own, doc_lengths[0])
    keys_all, values_all = (
        lax.all_gather(key_low, "ctx", axis=0, tiled=True),
        lax.all_gather(value_low, "ctx", axis=0, tiled=True),
    )
    places_all = jnp.arange(length_total, dtype=jnp.int32)
    segs_all = segment_of(places_all, doc_lengths[0])
    allowed = segs_own[:, None] == segs_all[None, :]
    head_outs = []
    log_list = []
    for head in range(H):
        cols = slice(head * HD, (head + 1) * HD)
        scores = masked_scores(query_low[:, cols], keys_all[:, cols], allowed, scale)
        top = jnp.max(scores, axis=1, keepdims=True)
        expd = jnp.exp(scores - top)
        total = jnp.sum(expd, axis=1, keepdims=True)
        probs_low = (expd / total).astype(jnp.bfloat16)
        head_outs.append(
            jnp.dot(probs_low, values_all[:, cols], preferred_element_type=jnp.float32)
        )
        log_list.append(top[:, 0] + jnp.log(total[:, 0]))
    attn_low = jnp.concatenate(head_outs, axis=1).astype(jnp.bfloat16)
    log_sums = jnp.stack(log_list, axis=0)
    branch = jnp.dot(attn_low, out_full, preferred_element_type=jnp.float32) + obias_full.astype(
        jnp.float32
    )
    hidden, first_back = jax.vjp(
        layer_norm,
        local_float + branch,
        gain_one.astype(jnp.float32),
        shift_one.astype(jnp.float32),
    )
    hidden_low = hidden.astype(jnp.bfloat16)
    inner = jnp.dot(hidden_low, inner_full, preferred_element_type=jnp.float32) + ibias_full.astype(
        jnp.float32
    )
    active, gelu_back = jax.vjp(gelu_exact, inner)
    active_low = active.astype(jnp.bfloat16)
    outer = jnp.dot(
        active_low, outer_full, preferred_element_type=jnp.float32
    ) + outbias_full.astype(jnp.float32)
    result, second_back = jax.vjp(
        layer_norm, hidden + outer, gain_two.astype(jnp.float32), shift_two.astype(jnp.float32)
    )
    output = result.astype(jnp.bfloat16)[None]
    grad_y = grad_output[0].astype(jnp.float32)
    d_second, grad_gain_two, grad_shift_two = second_back(grad_y)
    d_outer_low = d_second.astype(jnp.bfloat16)
    grad_outbias = jnp.sum(d_outer_low.astype(jnp.float32), axis=0)
    grad_outer = inner_cols(active_low, d_outer_low)
    d_active = inner_rows(d_outer_low, outer_full)
    (d_inner,) = gelu_back(d_active)
    d_inner_low = d_inner.astype(jnp.bfloat16)
    grad_ibias = jnp.sum(d_inner_low.astype(jnp.float32), axis=0)
    grad_inner = inner_cols(hidden_low, d_inner_low)
    d_hidden = d_second + inner_rows(d_inner_low, inner_full)
    d_first, grad_gain_one, grad_shift_one = first_back(d_hidden)
    d_branch_low = d_first.astype(jnp.bfloat16)
    grad_obias = jnp.sum(d_branch_low.astype(jnp.float32), axis=0)
    grad_out = inner_cols(attn_low, d_branch_low)
    d_attn_low = inner_rows(d_branch_low, out_full).astype(jnp.bfloat16)
    dq_list = []
    dk_list = []
    dv_list = []
    for head in range(H):
        cols = slice(head * HD, (head + 1) * HD)
        scores = masked_scores(query_low[:, cols], keys_all[:, cols], allowed, scale)
        probs = jnp.exp(scores - log_sums[head][:, None])
        d_probs = inner_rows(d_attn_low[:, cols], values_all[:, cols])
        delta = jnp.sum(probs * d_probs, axis=1)
        d_scores = (probs * (d_probs - delta[:, None])).astype(jnp.bfloat16)
        dq_list.append(
            jnp.dot(d_scores, keys_all[:, cols], preferred_element_type=jnp.float32) * scale
        )
        dk_list.append(inner_cols(d_scores, query_low[:, cols]) * scale)
        dv_list.append(inner_cols(probs.astype(jnp.bfloat16), d_attn_low[:, cols]))
    key_terms = jnp.concatenate(dk_list + dv_list, axis=1)
    shares = lax.psum_scatter(
        key_terms.astype(jnp.bfloat16), "ctx", scatter_dimension=0, tiled=True
    ).astype(jnp.float32)
    d_key_low = shares[:, :width].astype(jnp.bfloat16)
    d_value_low = shares[:, width:].astype(jnp.bfloat16)
    d_query_low = jnp.concatenate(dq_list, axis=1).astype(jnp.bfloat16)
    grad_qbias = jnp.sum(d_query_low.astype(jnp.float32), axis=0)
    grad_vbias = jnp.sum(d_value_low.astype(jnp.float32), axis=0)
    grad_query = inner_cols(local_in, d_query_low)
    grad_key = inner_cols(local_in, d_key_low)
    grad_value = inner_cols(local_in, d_value_low)
    grad_input = (
        d_first
        + inner_rows(d_query_low, query_full)
        + inner_rows(d_key_low, key_full)
        + inner_rows(d_value_low, value_full)
    )
    shards = (
        lax.psum_scatter(
            grad_query.astype(jnp.bfloat16), "fsdp", scatter_dimension=0, tiled=True
        ).astype(jnp.float32),
        lax.psum_scatter(
            grad_qbias.astype(jnp.bfloat16), "fsdp", scatter_dimension=0, tiled=True
        ).astype(jnp.float32),
        lax.psum_scatter(
            grad_key.astype(jnp.bfloat16), "fsdp", scatter_dimension=0, tiled=True
        ).astype(jnp.float32),
        lax.psum_scatter(
            grad_value.astype(jnp.bfloat16), "fsdp", scatter_dimension=0, tiled=True
        ).astype(jnp.float32),
        lax.psum_scatter(
            grad_vbias.astype(jnp.bfloat16), "fsdp", scatter_dimension=0, tiled=True
        ).astype(jnp.float32),
        lax.psum_scatter(
            grad_out.astype(jnp.bfloat16), "fsdp", scatter_dimension=0, tiled=True
        ).astype(jnp.float32),
        lax.psum_scatter(
            grad_obias.astype(jnp.bfloat16), "fsdp", scatter_dimension=0, tiled=True
        ).astype(jnp.float32),
        lax.psum_scatter(
            grad_gain_one.astype(jnp.bfloat16), "fsdp", scatter_dimension=0, tiled=True
        ).astype(jnp.float32),
        lax.psum_scatter(
            grad_shift_one.astype(jnp.bfloat16), "fsdp", scatter_dimension=0, tiled=True
        ).astype(jnp.float32),
        lax.psum_scatter(
            grad_inner.astype(jnp.bfloat16), "fsdp", scatter_dimension=0, tiled=True
        ).astype(jnp.float32),
        lax.psum_scatter(
            grad_ibias.astype(jnp.bfloat16), "fsdp", scatter_dimension=0, tiled=True
        ).astype(jnp.float32),
        lax.psum_scatter(
            grad_outer.astype(jnp.bfloat16), "fsdp", scatter_dimension=0, tiled=True
        ).astype(jnp.float32),
        lax.psum_scatter(
            grad_outbias.astype(jnp.bfloat16), "fsdp", scatter_dimension=0, tiled=True
        ).astype(jnp.float32),
        lax.psum_scatter(
            grad_gain_two.astype(jnp.bfloat16), "fsdp", scatter_dimension=0, tiled=True
        ).astype(jnp.float32),
        lax.psum_scatter(
            grad_shift_two.astype(jnp.bfloat16), "fsdp", scatter_dimension=0, tiled=True
        ).astype(jnp.float32),
    )
    totals = lax.psum(tuple(shards), "ctx")
    return (output, grad_input[None]) + tuple(totals)


def solution(mesh):
    placed = (
        P("fsdp", "ctx", None),
        P("fsdp", None),
        P("fsdp"),
        P("fsdp", None),
        P("fsdp", None),
        P("fsdp"),
        P("fsdp", None),
        P("fsdp"),
        P("fsdp"),
        P("fsdp"),
        P("fsdp", None),
        P("fsdp"),
        P("fsdp", None),
        P("fsdp"),
        P("fsdp"),
        P("fsdp"),
        P("fsdp", None),
        P("fsdp", "ctx", None),
    )
    return jax.shard_map(
        on_device,
        mesh=mesh,
        in_specs=placed,
        out_specs=(
            P("fsdp", "ctx", None),
            P("fsdp", "ctx", None),
            P("fsdp", None),
            P("fsdp"),
            P("fsdp", None),
            P("fsdp", None),
            P("fsdp"),
            P("fsdp", None),
            P("fsdp"),
            P("fsdp"),
            P("fsdp"),
            P("fsdp", None),
            P("fsdp"),
            P("fsdp", None),
            P("fsdp"),
            P("fsdp"),
            P("fsdp"),
        ),
        check_vma=False,
    )
```

profile of v0, /device:TPU:1, one launch (start us, length us, event | category | flops | bytes accessed | tf_op | source)
XLA Modules:
  0.0 1196.2 jit_solution(10272641338332044763)
XLA Ops:
  9.5 25.0 %all-gather.20.cloned.1.call-done = bf16[768,768]{1,0:T(8,128)(2,1)} async-done(((bf16[384,768]{1,0:T(8,128)(2,1)}), bf16[768,768]{1,0:T(8,128)(2,1)}) %all-gather.20.cloned.1.call-update) | async-done | bytes 1179664 | tf_op jit(solution)/shard_map/all_gather | solution.py:72
  41.2 17.6 %all-gather.24.cloned.1.call-done = bf16[768,768]{1,0:T(8,128)(2,1)} async-done(((bf16[384,768]{1,0:T(8,128)(2,1)}), bf16[768,768]{1,0:T(8,128)(2,1)}) %all-gather.24.cloned.1.call-update) | async-done | bytes 1179664 | tf_op jit(solution)/shard_map/all_gather | solution.py:73
  93.4 54.9 %all-gather.22.cloned.1.call-done = bf16[4096,768]{1,0:T(8,128)(2,1)} async-done(((bf16[256,768]{1,0:T(8,128)(2,1)}), bf16[4096,768]{1,0:T(8,128)(2,1)}) %all-gather.22.cloned.1.call-update) | async-done | bytes 6291472 | tf_op jit(solution)/shard_map/all_gather | solution.py:118
  194.7 16.8 %all-gather.26.cloned.1.call-done = bf16[4096,768]{1,0:T(8,128)(2,1)} async-done(((bf16[256,768]{1,0:T(8,128)(2,1)}), bf16[4096,768]{1,0:T(8,128)(2,1)}) %all-gather.26.cloned.1.call-update) | async-done | bytes 6291472 | tf_op jit(solution)/shard_map/all_gather | solution.py:119
  243.4 54.8 %all-gather.30.cloned.1.call-done = bf16[768,3072]{1,0:T(8,128)(2,1)} async-done(((bf16[384,3072]{1,0:T(8,128)(2,1)}), bf16[768,3072]{1,0:T(8,128)(2,1)}) %all-gather.30.cloned.1.call-update) | async-done | bytes 4718608 | tf_op jit(solution)/shard_map/all_gather | solution.py:79
  298.2 11.5 multiply_convert_fusion.12
  309.7 52.7 %all-gather.32.cloned.1.call-done = bf16[3072,768]{1,0:T(8,128)(2,1)} async-done(((bf16[1536,768]{1,0:T(8,128)(2,1)}), bf16[3072,768]{1,0:T(8,128)(2,1)}) %all-gather.32.cloned.1.call-update) | async-done | bytes 4718608 | tf_op jit(solution)/shard_map/all_gather | solution.py:81
  392.8 4.9 multiply_convert_fusion.8
  400.7 4.9 multiply_convert_fusion.7
  405.5 4.4 multiply_reduce_fusion.6
  410.0 4.9 multiply_convert_fusion.6
  419.0 4.8 multiply_convert_fusion.5
  423.8 5.6 multiply_reduce_fusion.4
  429.4 6.4 multiply_convert_fusion.4
  435.8 5.3 multiply_reduce_fusion.3
  441.1 6.0 multiply_convert_fusion.3
  447.1 5.6 multiply_reduce_fusion.2
  452.6 5.9 multiply_convert_fusion.2
  458.6 5.3 multiply_reduce_fusion.1
  463.9 6.0 multiply_convert_fusion.1
  469.9 5.6 multiply_reduce_fusion
  475.5 5.9 multiply_convert_fusion
  549.4 5.2 convolution_convert_fusion.1
  560.3 93.9 %reduce-scatter.14.cloned.1.call-done = bf16[256,1536]{0,1:T(8,128)(2,1)} async-done(((bf16[4096,1536]{0,1:T(8,128)(2,1)}), bf16[256,1536]{0,1:T(8,128)(2,1)}) %reduce-scatter.14.cloned.1.call-update) | async-done | bytes 786448 | tf_op jit(solution)/shard_map/reduce_scatter | solution.py:193
  668.9 9.7 reduce-scatter.22.cloned.1.call-done
  679.9 22.8 %reduce-scatter.16.cloned.1.call-done = bf16[384,768]{1,0:T(8,128)(2,1)} async-done(((bf16[768,768]{1,0:T(8,128)(2,1)}), bf16[384,768]{1,0:T(8,128)(2,1)}) %reduce-scatter.16.cloned.1.call-update) | async-done | bytes 589840 | tf_op jit(solution)/shard_map/reduce_scatter | solution.py:226
  702.7 62.7 %reduce-scatter.18.cloned.1.call-done = bf16[384,3072]{1,0:T(8,128)(2,1)} async-done(((bf16[768,3072]{1,0:T(8,128)(2,1)}), bf16[384,3072]{1,0:T(8,128)(2,1)}) %reduce-scatter.18.cloned.1.call-update) | async-done | bytes 2359312 | tf_op jit(solution)/shard_map/reduce_scatter | solution.py:238
  765.4 63.0 %reduce-scatter.20.cloned.1.call-done = bf16[1536,768]{1,0:T(8,128)(2,1)} async-done(((bf16[3072,768]{1,0:T(8,128)(2,1)}), bf16[1536,768]{1,0:T(8,128)(2,1)}) %reduce-scatter.20.cloned.1.call-update) | async-done | bytes 2359312 | tf_op jit(solution)/shard_map/reduce_scatter | solution.py:244
  828.6 6.1 all-reduce.10
  841.4 11.6 reduce-scatter.24.cloned.1.call-done
  854.4 23.1 %reduce-scatter.26.cloned.1.call-done = bf16[384,768]{1,0:T(8,128)(2,1)} async-done(((bf16[768,768]{1,0:T(8,128)(2,1)}), bf16[384,768]{1,0:T(8,128)(2,1)}) %reduce-scatter.26.cloned.1.call-update) | async-done | bytes 589840
  878.8 303.9 %all-reduce.12 = (f32[384,768]{0,1:T(8,128)}, f32[384]{0:T(512)}, f32[384,768]{0,1:T(8,128)}, f32[384,768]{0,1:T(8,128)S(1)}, f32[384]{0:T(512)}, /*index=5*/f32...) all-reduce(bf16[384,768]{0,1:T(8,128)(2,1)S(1)} %copy.52, ...), channel_id=1, replica_groups=mesh['ctx'=16,'fsdp'=2] {'ctx'}, use_global_device_ids=true, to_apply=%region_49.50 | all-reduce | flops 3543552 | bytes 21270528 | tf_op jit(solution)/shard_map/psum | solution.py:257
  (419 shorter events, 263.0 us)
Async XLA Ops:
  7.2 27.3 %all-gather.20.cloned.1.call-start = ((), (), s32[]{:S(2)}) async-start(), calls=%async_computation.8 | async-start | bytes 1769472 | tf_op jit(solution)/shard_map/all_gather | solution.py:72
  7.9 50.9 %all-gather.24.cloned.1.call-start = ((), (), s32[]{:S(2)}) async-start(), calls=%async_computation.10 | async-start | bytes 1769472 | tf_op jit(solution)/shard_map/all_gather | solution.py:73
  8.7 82.9 %all-gather.18.cloned.1.call-start = ((), (), s32[]{:S(2)}) async-start(), calls=%async_computation.7 | async-start | bytes 1769472 | tf_op jit(solution)/shard_map/all_gather | solution.py:70
  9.4 138.9 %all-gather.22.cloned.1.call-start = ((), (), s32[]{:S(2)}) async-start(), calls=%async_computation.9 | async-start | bytes 6684672 | tf_op jit(solution)/shard_map/all_gather | solution.py:118
  37.1 26.5 %copy-start.82 = (bf16[384]{0:T(512)(128)(2,1)S(1)}, bf16[384]{0:T(512)(128)(2,1)}, u32[]{:S(2)}) copy-start(bf16[384]{0:T(512)(128)(2,1)} %param.31) | copy-start | bytes 2308
  37.1 29.7 %copy-start.81 = (bf16[1536]{0:T(1024)(128)(2,1)S(1)}, bf16[1536]{0:T(1024)(128)(2,1)}, u32[]{:S(2)}) copy-start(bf16[1536]{0:T(1024)(128)(2,1)} %param.29) | copy-start | bytes 9220
  37.1 33.0 %copy-start.83 = (bf16[384]{0:T(512)(128)(2,1)S(1)}, bf16[384]{0:T(512)(128)(2,1)}, u32[]{:S(2)}) copy-start(bf16[384]{0:T(512)(128)(2,1)} %param.25) | copy-start | bytes 2308
  37.1 36.6 %copy-start.84 = (bf16[384]{0:T(512)(128)(2,1)S(1)}, bf16[384]{0:T(512)(128)(2,1)}, u32[]{:S(2)}) copy-start(bf16[384]{0:T(512)(128)(2,1)} %param.20) | copy-start | bytes 2308
  37.1 40.1 %copy-start.89 = (s32[1,48]{1,0:T(1,128)S(1)}, s32[1,48]{1,0:T(1,128)}, u32[]{:S(2)}) copy-start(s32[1,48]{1,0:T(1,128)} %param.34) | copy-start | bytes 580
  37.1 40.7 %copy-start.85 = (bf16[384]{0:T(512)(128)(2,1)S(1)}, bf16[384]{0:T(512)(128)(2,1)}, u32[]{:S(2)}) copy-start(bf16[384]{0:T(512)(128)(2,1)} %param.27) | copy-start | bytes 2308
  37.1 44.2 %copy-start.86 = (bf16[384]{0:T(512)(128)(2,1)S(1)}, bf16[384]{0:T(512)(128)(2,1)}, u32[]{:S(2)}) copy-start(bf16[384]{0:T(512)(128)(2,1)} %param.26) | copy-start | bytes 2308
  37.2 47.4 %copy-start.87 = (bf16[384]{0:T(512)(128)(2,1)S(1)}, bf16[384]{0:T(512)(128)(2,1)}, u32[]{:S(2)}) copy-start(bf16[384]{0:T(512)(128)(2,1)} %param.32) | copy-start | bytes 2308
  37.2 50.7 %copy-start.88 = (bf16[384]{0:T(512)(128)(2,1)S(1)}, bf16[384]{0:T(512)(128)(2,1)}, u32[]{:S(2)}) copy-start(bf16[384]{0:T(512)(128)(2,1)} %param.33) | copy-start | bytes 2308
  37.2 54.4 %copy-start.57 = (bf16[1,256,768]{2,1,0:T(8,128)(2,1)S(1)}, bf16[1,256,768]{2,1,0:T(8,128)(2,1)}, u32[]{:S(2)}) copy-start(bf16[1,256,768]{2,1,0:T(8,128)(2,1)} %param.18) | copy-start | bytes 1179652
  37.2 174.3 %all-gather.26.cloned.1.call-start = ((), (), s32[]{:S(2)}) async-start(), calls=%async_computation.11 | async-start | bytes 6684672 | tf_op jit(solution)/shard_map/all_gather | solution.py:119
  61.5 179.4 %all-gather.28.cloned.1.call-start = ((), (), s32[]{:S(2)}) async-start(), calls=%async_computation.12 | async-start | bytes 1769472 | tf_op jit(solution)/shard_map/all_gather | solution.py:75
  62.0 236.2 %all-gather.30.cloned.1.call-start = ((), (), s32[]{:S(2)}) async-start(), calls=%async_computation.13 | async-start | bytes 7077888 | tf_op jit(solution)/shard_map/all_gather | solution.py:79
  62.8 299.6 %all-gather.32.cloned.1.call-start = ((), (), s32[]{:S(2)}) async-start(), calls=%async_computation.14 | async-start | bytes 7077888 | tf_op jit(solution)/shard_map/all_gather | solution.py:81
  63.5 590.6 %reduce-scatter.14.cloned.1.call-start = ((), (), s32[]{:S(2)}) async-start(), calls=%async_computation.15 | async-start | bytes 13369344 | tf_op jit(solution)/shard_map/reduce_scatter | solution.py:193
  93.4 57.8 %copy-start.78 = (bf16[256,768]{1,0:T(8,128)(2,1)}, bf16[256,768]{1,0:T(8,128)(2,1)S(1)}, u32[]{:S(2)}) copy-start(bf16[256,768]{1,0:T(8,128)(2,1)S(1)} %fusion.108) | copy-start | bytes 1179652
  240.9 57.3 %copy-start.75 = (bf16[256,768]{0,1:T(8,128)(2,1)}, bf16[256,768]{0,1:T(8,128)(2,1)S(1)}, u32[]{:S(2)}) copy-start(bf16[256,768]{0,1:T(8,128)(2,1)S(1)} %fusion.157) | copy-start | bytes 1179652
  309.7 56.7 %copy-start.69 = (bf16[256,3072]{1,0:T(8,128)(2,1)}, bf16[256,3072]{1,0:T(8,128)(2,1)S(1)}, u32[]{:S(2)}) copy-start(bf16[256,3072]{1,0:T(8,128)(2,1)S(1)} %get-tuple-element.124) | copy-start | bytes 4718596
  377.3 28.2 %copy-start.59 = (bf16[256,768]{1,0:T(8,128)(2,1)}, bf16[256,768]{1,0:T(8,128)(2,1)S(1)}, u32[]{:S(2)}) copy-start(bf16[256,768]{1,0:T(8,128)(2,1)S(1)} %convolution_convert_fusion.18) | copy-start | bytes 1179652
  520.1 158.4 %reduce-scatter.22.cloned.1.call-start = ((), (), s32[]{:S(2)}) async-start(), calls=%async_computation.19 | async-start | bytes 1769472
  521.7 16.8 %slice-start = ((s8[6291456]{0:T(1024)(128)(4,1)}), s8[4194304]{0:T(1024)(128)(4,1)S(1)}, s32[]{:S(2)}) async-start(s8[6291456]{0:T(1024)(128)(4,1)} %bitcast.84), calls=%async_computation.22 | async-start | bytes 8388608
  547.7 155.0 %reduce-scatter.16.cloned.1.call-start = ((), (), s32[]{:S(2)}) async-start(), calls=%async_computation.16 | async-start | bytes 1769472 | tf_op jit(solution)/shard_map/reduce_scatter | solution.py:226
  549.3 216.1 %reduce-scatter.18.cloned.1.call-start = ((), (), s32[]{:S(2)}) async-start(), calls=%async_computation.17 | async-start | bytes 7077888 | tf_op jit(solution)/shard_map/reduce_scatter | solution.py:238
  554.6 273.9 %reduce-scatter.20.cloned.1.call-start = ((), (), s32[]{:S(2)}) async-start(), calls=%async_computation.18 | async-start | bytes 7077888 | tf_op jit(solution)/shard_map/reduce_scatter | solution.py:244
  560.2 292.7 %reduce-scatter.24.cloned.1.call-start = ((), (), s32[]{:S(2)}) async-start(), calls=%async_computation.20 | async-start | bytes 1769472
  657.2 220.3 %reduce-scatter.26.cloned.1.call-start = ((), (), s32[]{:S(2)}) async-start(), calls=%async_computation.21 | async-start | bytes 1769472
  658.7 178.1 %copy-start.64 = (bf16[768,768]{1,0:T(8,128)(2,1)S(1)}, bf16[768,768]{1,0:T(8,128)(2,1)}, u32[]{:S(2)}) copy-start(bf16[768,768]{1,0:T(8,128)(2,1)} %all-gather.20.cloned.1.call-done) | copy-start | bytes 3538948
  838.6 40.2 %copy-start.80 = (bf16[384,768]{1,0:T(8,128)(2,1)S(1)}, bf16[384,768]{1,0:T(8,128)(2,1)}, u32[]{:S(2)}) copy-start(bf16[384,768]{1,0:T(8,128)(2,1)} %reduce-scatter.16.cloned.1.call-done) | copy-start | bytes 1769476
  (83 other events, 346.8 us)
Sparse Core Ops, SparseCore 0:
  9.6 24.8 all-gather.19
  36.0 22.7 all-gather.23
  60.4 22.9 all-gather.17
  86.0 62.2 all-gather.21
  151.0 60.4 all-gather.25
  212.9 20.9 all-gather.27
  235.5 62.6 all-gather.29
  299.7 62.5 all-gather.31
  520.3 133.8 reduce-scatter.13
  656.8 21.6 reduce-scatter.21
  680.9 21.7 reduce-scatter.15
  705.4 59.9 reduce-scatter.17
  768.4 59.9 reduce-scatter.19
  831.1 21.8 reduce-scatter.23
  855.8 21.6 reduce-scatter.25
where the time goes:
time: 1200 us
  waiting for transfers between devices  513 us (43%)
  blocking collectives  340 us (28%)
  matrix products  214 us (18%)
  other arithmetic  72.8 us (6%)
  local copies, waits for them, and re-layouts  38.5 us (3%)
  between operations  16.7 us (1%)
    psum x1, blocking collectives, on_device(): totals = lax.psum(tuple(shards), 'ctx')  304 us
    dot_general x30, matrix products, inner_rows(): lax.dot_general(left, right, (((1,), (1,)), ((), ())), preferred_element_...  94 us
    reduce_scatter x1, waiting for transfers between devices, on_device(): lax.psum_scatter(key_terms.astype(jnp.bfloat16), 'ctx', scatter_dimension...  93.9 us
    reduce_scatter x1, waiting for transfers between devices, on_device(): lax.psum_scatter(grad_outer.astype(jnp.bfloat16), 'fsdp', scatter_dimensi...  63 us
    reduce_scatter x1, waiting for transfers between devices, on_device(): lax.psum_scatter(grad_inner.astype(jnp.bfloat16), 'fsdp', scatter_dimensi...  62.7 us
    convert_element_type x12, other arithmetic, on_device(): d_scores = (probs * (d_probs - delta[:, None])).astype(jnp.bfloat16)  56.2 us
    all_gather x1, waiting for transfers between devices, on_device(): lax.all_gather(key_low, 'ctx', axis=0, tiled=True)  54.9 us
    all_gather x1, waiting for transfers between devices, on_device(): lax.all_gather(inner_weight, 'fsdp', axis=0, tiled=True)  54.8 us
  transfers between devices with their start and end apart: 15, of which 13 were waited for; matrix products, arithmetic and copies ran while one was open for 12% of the time, Pallas kernels for 0%

commit v1 on v0

--- a/solution.py
+++ b/solution.py
@@ -7,6 +7,28 @@
 H = 12
 HD = 64
 eps = 1e-12
+
+
+def laid_out(blocks, dim):
+    dims = list(blocks.shape[1:])
+    dims[dim] *= blocks.shape[0]
+    return jnp.moveaxis(blocks, 0, dim).reshape(dims)
+
+
+def gather_around(array, axis, dim):
+    size = lax.axis_size(axis)
+    pairs = [(i, (i + 1) % size) for i in range(size)]
+    back = [(b, a) for a, b in pairs]
+    lower, upper = ([], [])
+    for step in range(size - 1):
+        if step % 2 == 0:
+            lower.append(lax.ppermute(lower[-1] if lower else array, axis, pairs))
+        else:
+            upper.append(lax.ppermute(upper[-1] if upper else array, axis, back))
+    blocks = jnp.stack([*lower[::-1], array, *upper])
+    shift = lax.axis_index(axis) - len(lower)
+    blocks = blocks[(jnp.arange(size) - shift) % size]
+    return laid_out(blocks, dim)
 
 
 def layer_norm(r, gain, shift):
@@ -115,7 +137,7 @@
     places_own = first_row + jnp.arange(rows, dtype=jnp.int32)
     segs_own = segment_of(places_own, doc_lengths[0])
     keys_all, values_all = (
-        lax.all_gather(key_low, "ctx", axis=0, tiled=True),
+        gather_around(key_low, "ctx", 0),
         lax.all_gather(value_low, "ctx", axis=0, tiled=True),
     )
     places_all = jnp.arange(length_total, dtype=jnp.int32)

time: 1200 us -> 1130 us (0.942)
  waiting for transfers between devices: 513 us -> 430 us
  matrix products: 214 us -> 186 us
  local copies, waits for them, and re-layouts: 38.5 us -> 64 us
  starting transfers between devices: 1.07 us -> 24.9 us
  other arithmetic: 72.8 us -> 60 us
    all_gather x1 -> x0, waiting for transfers between devices: 54.9 us -> none  [on_device(): lax.all_gather(key_low, 'ctx', axis=0, tiled=True)]
    all_gather x1, waiting for transfers between devices: 54.8 us -> 0.02 us  [on_device(): lax.all_gather(inner_weight, 'fsdp', axis=0, tiled=True)]
    ppermute x0 -> x15, waiting for transfers between devices: none -> 50.8 us  [the longest x8 32.5 us: gather_around(): lower.append(lax.ppermute(lower[-1] if lower else array, axis, pairs))]
    dot_general x30, matrix products: 94 us -> 66.3 us  [inner_rows(): lax.dot_general(left, right, (((1,), (1,)), ((), ())), preferred_element_...]
    ppermute x0 -> x15, starting transfers between devices: none -> 23.9 us  [the longest x8 20.2 us: gather_around(): lower.append(lax.ppermute(lower[-1] if lower else array, axis, pairs))]
    convert_element_type x12, other arithmetic: 56.2 us -> 34.9 us  [on_device(): d_scores = (probs * (d_probs - delta[:, None])).astype(jnp.bfloat16)]
    unnamed x219 -> x248, local copies, waits for them, and re-layouts: 38.3 us -> 56.7 us
    all_gather x1, waiting for transfers between devices: 16.8 us -> 0.01 us  [on_device(): lax.all_gather(value_low, 'ctx', axis=0, tiled=True)]
  transfers between devices with their start and end apart: 15 -> 29, of which waited for: 13 -> 19; matrix products, arithmetic and copies ran while one was open for 12% -> 14% of each run, Pallas kernels for 0% -> 0%
where the time goes in v1:
time: 1130 us; the launch traced here: 1120 us
  waiting for transfers between devices  430 us (38%)
  blocking collectives  341 us (30%)
  matrix products  186 us (16%)
  local copies, waits for them, and re-layouts  64 us (6%)
  other arithmetic  60 us (5%)
  starting transfers between devices  24.9 us (2%)
  between operations  16.8 us (1%)
    psum x1, blocking collectives, on_device(): totals = lax.psum(tuple(shards), 'ctx')  304 us
    reduce_scatter x1, waiting for transfers between devices, on_device(): lax.psum_scatter(key_terms.astype(jnp.bfloat16), 'ctx', scatter_dimension...  93.8 us
    dot_general x30, matrix products, inner_rows(): lax.dot_general(left, right, (((1,), (1,)), ((), ())), preferred_element_...  66.3 us
    reduce_scatter x1, waiting for transfers between devices, on_device(): lax.psum_scatter(grad_inner.astype(jnp.bfloat16), 'fsdp', scatter_dimensi...  62.9 us
    reduce_scatter x1, waiting for transfers between devices, on_device(): lax.psum_scatter(grad_outer.astype(jnp.bfloat16), 'fsdp', scatter_dimensi...  62.9 us
    unnamed x248, local copies, waits for them, and re-layouts  56.7 us
    dot_general x30, matrix products, inner_cols(): lax.dot_general(left, right, (((0,), (0,)), ((), ())), preferred_element_...  55.1 us
    unnamed x17, waiting for transfers between devices  48 us
  transfers between devices with their start and end apart: 29, of which 19 were waited for; matrix products, arithmetic and copies ran while one was open for 14% of the time, Pallas kernels for 0%

profile of v1, /device:TPU:1, one launch (start us, length us, event | category | flops | bytes accessed | tf_op | source)
XLA Modules:
  0.0 1122.6 jit_solution(8759589027572472324)
XLA Ops:
  13.9 20.5 %all-gather.21.cloned.1.call-done = bf16[768,768]{1,0:T(8,128)(2,1)} async-done(((bf16[384,768]{1,0:T(8,128)(2,1)}), bf16[768,768]{1,0:T(8,128)(2,1)}) %all-gather.21.cloned.1.call-update) | async-done | bytes 1179664 | tf_op jit(solution)/shard_map/all_gather | solution.py:95
  38.4 20.4 %all-gather.19.cloned.1.call-done = bf16[768,768]{1,0:T(8,128)(2,1)} async-done(((bf16[384,768]{1,0:T(8,128)(2,1)}), bf16[768,768]{1,0:T(8,128)(2,1)}) %all-gather.19.cloned.1.call-update) | async-done | bytes 1179664 | tf_op jit(solution)/shard_map/all_gather | solution.py:94
  62.4 4.7 collective-permute-done
  71.2 7.3 collective-permute-done.1
  81.4 8.5 collective-permute-done.2
  92.8 11.9 %collective-permute-done.3 = bf16[256,768]{1,0:T(8,128)(2,1)} collective-permute-done((bf16[256,768]{1,0:T(8,128)(2,1)S(1)}, bf16[256,768]{1,0:T(8,128)(2,1)}, u32[]{:S(2)}, u32[]{:S(2)}) %collective-permute-start.3) | collective-permute-done | bytes 393248 | tf_op jit(solution)/shard_map/ppermute | solution.py:25
  135.6 7.8 collective-permute-done.11
  143.4 4.2 collective-permute-start.6
  151.7 3.9 collective-permute-done.12
  159.6 5.8 collective-permute-done.13
  186.0 6.3 gather_fusion
  192.3 4.2 fusion.294
  196.5 4.3 fusion.295
  213.4 5.8 fusion.36
  262.0 11.7 %multiply_convert_fusion.12 = (bf16[256,3072]{1,0:T(8,128)(2,1)S(1)}, f32[256,3072]{1,0:T(8,128)}, f32[256,3072]{1,0:T(8,128)}) fusion(f32[3072]{0:T(1024)S(1)} %bitcast.145, bf16[768,3072]{1,0:T(8,128)(2,1)} %all-gather.27.cloned.1.call-done, f32[256,768]{1,0:T(8,128)S(1)} %get-tuple-element.152, f32[768]{0:T(1024)S(1)} %reshape.329, ...), kind=kOutput, calls=%fused_computation.175 | convolution fusion | flops 1260847104 | bytes 13389824 | tf_op jit(solution)/shard_map/dot_general | solution.py:171
  273.7 47.9 %all-gather.29.cloned.1.call-done = bf16[3072,768]{1,0:T(8,128)(2,1)} async-done(((bf16[1536,768]{1,0:T(8,128)(2,1)}), bf16[3072,768]{1,0:T(8,128)(2,1)}) %all-gather.29.cloned.1.call-update) | async-done | bytes 4718608 | tf_op jit(solution)/shard_map/all_gather | solution.py:103
  321.7 4.0 fusion.307
  389.1 4.2 multiply_reduce_fusion.1
  393.3 4.9 multiply_convert_fusion.1
  398.2 4.4 multiply_reduce_fusion
  402.6 4.8 multiply_convert_fusion
  450.1 4.1 fusion.113
  475.6 5.2 convolution_convert_fusion.1
  486.5 93.8 %reduce-scatter.14.cloned.1.call-done = bf16[256,1536]{0,1:T(8,128)(2,1)} async-done(((bf16[4096,1536]{0,1:T(8,128)(2,1)}), bf16[256,1536]{0,1:T(8,128)(2,1)}) %reduce-scatter.14.cloned.1.call-update) | async-done | bytes 786448 | tf_op jit(solution)/shard_map/reduce_scatter | solution.py:215
  595.1 9.8 reduce-scatter.22.cloned.1.call-done
  606.3 22.6 %reduce-scatter.16.cloned.1.call-done = bf16[384,768]{1,0:T(8,128)(2,1)} async-done(((bf16[768,768]{1,0:T(8,128)(2,1)}), bf16[384,768]{1,0:T(8,128)(2,1)}) %reduce-scatter.16.cloned.1.call-update) | async-done | bytes 589840 | tf_op jit(solution)/shard_map/reduce_scatter | solution.py:248
  628.9 62.9 %reduce-scatter.18.cloned.1.call-done = bf16[384,3072]{1,0:T(8,128)(2,1)} async-done(((bf16[768,3072]{1,0:T(8,128)(2,1)}), bf16[384,3072]{1,0:T(8,128)(2,1)}) %reduce-scatter.18.cloned.1.call-update) | async-done | bytes 2359312 | tf_op jit(solution)/shard_map/reduce_scatter | solution.py:260
  691.8 62.9 %reduce-scatter.20.cloned.1.call-done = bf16[1536,768]{1,0:T(8,128)(2,1)} async-done(((bf16[3072,768]{1,0:T(8,128)(2,1)}), bf16[1536,768]{1,0:T(8,128)(2,1)}) %reduce-scatter.20.cloned.1.call-update) | async-done | bytes 2359312 | tf_op jit(solution)/shard_map/reduce_scatter | solution.py:266
  754.8 6.1 all-reduce.10
  767.6 11.7 %reduce-scatter.24.cloned.1.call-done = bf16[384,768]{1,0:T(8,128)(2,1)} async-done(((bf16[768,768]{1,0:T(8,128)(2,1)}), bf16[384,768]{1,0:T(8,128)(2,1)}) %reduce-scatter.24.cloned.1.call-update) | async-done | bytes 589840
  780.6 23.2 %reduce-scatter.26.cloned.1.call-done = bf16[384,768]{1,0:T(8,128)(2,1)} async-done(((bf16[768,768]{1,0:T(8,128)(2,1)}), bf16[384,768]{1,0:T(8,128)(2,1)}) %reduce-scatter.26.cloned.1.call-update) | async-done | bytes 589840
  805.2 303.9 %all-reduce.12 = (f32[384,768]{0,1:T(8,128)}, f32[384]{0:T(512)}, f32[384,768]{0,1:T(8,128)}, f32[384,768]{0,1:T(8,128)S(1)}, f32[384]{0:T(512)}, /*index=5*/f32...) all-reduce(bf16[384,768]{0,1:T(8,128)(2,1)S(1)} %copy.52, ...), channel_id=1, replica_groups=mesh['ctx'=16,'fsdp'=2] {'ctx'}, use_global_device_ids=true, to_apply=%region_49.50 | all-reduce | flops 3543552 | bytes 21270528 | tf_op jit(solution)/shard_map/psum | solution.py:279
  (478 shorter events, 302.0 us)
Async XLA Ops:
  7.2 27.3 %all-gather.21.cloned.1.call-start = ((), (), s32[]{:S(2)}) async-start(), calls=%async_computation.9 | async-start | bytes 1769472 | tf_op jit(solution)/shard_map/all_gather | solution.py:95
  7.9 50.9 %all-gather.19.cloned.1.call-start = ((), (), s32[]{:S(2)}) async-start(), calls=%async_computation.8 | async-start | bytes 1769472 | tf_op jit(solution)/shard_map/all_gather | solution.py:94
  8.7 149.1 %all-gather.17.cloned.1.call-start = ((), (), s32[]{:S(2)}) async-start(), calls=%async_computation.7 | async-start | bytes 1769472 | tf_op jit(solution)/shard_map/all_gather | solution.py:92
  9.4 221.2 %all-gather.23.cloned.1.call-start = ((), (), s32[]{:S(2)}) async-start(), calls=%async_computation.10 | async-start | bytes 6684672 | tf_op jit(solution)/shard_map/all_gather | solution.py:141
  37.2 110.4 %copy-start.90 = (bf16[1536]{0:T(1024)(128)(2,1)S(1)}, bf16[1536]{0:T(1024)(128)(2,1)}, u32[]{:S(2)}) copy-start(bf16[1536]{0:T(1024)(128)(2,1)} %param.29) | copy-start | bytes 9220
  37.2 114.0 %copy-start.98 = (s32[1,48]{1,0:T(1,128)S(1)}, s32[1,48]{1,0:T(1,128)}, u32[]{:S(2)}) copy-start(s32[1,48]{1,0:T(1,128)} %param.34) | copy-start | bytes 580
  37.2 222.5 %all-gather.25.cloned.1.call-start = ((), (), s32[]{:S(2)}) async-start(), calls=%async_computation.11 | async-start | bytes 1769472 | tf_op jit(solution)/shard_map/all_gather | solution.py:97
  37.8 224.1 %all-gather.27.cloned.1.call-start = ((), (), s32[]{:S(2)}) async-start(), calls=%async_computation.12 | async-start | bytes 7077888 | tf_op jit(solution)/shard_map/all_gather | solution.py:101
  38.4 283.3 %all-gather.29.cloned.1.call-start = ((), (), s32[]{:S(2)}) async-start(), calls=%async_computation.13 | async-start | bytes 7077888 | tf_op jit(solution)/shard_map/all_gather | solution.py:103
  60.6 6.5 collective-permute-start
  67.1 11.4 %collective-permute-start.1 = (bf16[256,768]{1,0:T(8,128)(2,1)S(1)}, bf16[256,768]{1,0:T(8,128)(2,1)S(1)}, u32[]{:S(2)}, u32[]{:S(2)}) collective-permute-start(bf16[256,768]{1,0:T(8,128)(2,1)S(1)} %collective-permute-done), channel_id=1, source_target_pairs={{0,2},{2,4},{4,6},{6,8},{8,10},{10,12},{12,14},{14,16},{16,18},{18... | collective-permute-start | bytes 1179656 | tf_op jit(solution)/shard_map/ppermute | solution.py:25
  69.6 11.8 %collective-permute-start.8 = (bf16[256,768]{1,0:T(8,128)(2,1)S(1)}, bf16[256,768]{1,0:T(8,128)(2,1)S(1)}, u32[]{:S(2)}, u32[]{:S(2)}) collective-permute-start(bf16[256,768]{1,0:T(8,128)(2,1)S(1)} %convolution_convert_fusion.19), channel_id=1, source_target_pairs={{2,0},{4,2},{6,4},{8,6},{10,8},{12,10},{14,12},{16,14},{18,16},{20... | collective-permute-start | bytes 1179656 | tf_op jit(solution)/shard_map/ppermute | solution.py:27
  78.5 11.4 %collective-permute-start.2 = (bf16[256,768]{1,0:T(8,128)(2,1)S(1)}, bf16[256,768]{1,0:T(8,128)(2,1)S(1)}, u32[]{:S(2)}, u32[]{:S(2)}) collective-permute-start(bf16[256,768]{1,0:T(8,128)(2,1)S(1)} %collective-permute-done.1), channel_id=1, source_target_pairs={{0,2},{2,4},{4,6},{6,8},{8,10},{10,12},{12,14},{14,16},{16,18},{18... | collective-permute-start | bytes 1179656 | tf_op jit(solution)/shard_map/ppermute | solution.py:25
  81.4 11.4 %collective-permute-start.9 = (bf16[256,768]{1,0:T(8,128)(2,1)S(1)}, bf16[256,768]{1,0:T(8,128)(2,1)S(1)}, u32[]{:S(2)}, u32[]{:S(2)}) collective-permute-start(bf16[256,768]{1,0:T(8,128)(2,1)S(1)} %collective-permute-done.8), channel_id=1, source_target_pairs={{2,0},{4,2},{6,4},{8,6},{10,8},{12,10},{14,12},{16,14},{18,16},{20... | collective-permute-start | bytes 1179656 | tf_op jit(solution)/shard_map/ppermute | solution.py:27
  89.9 14.8 %collective-permute-start.3 = (bf16[256,768]{1,0:T(8,128)(2,1)S(1)}, bf16[256,768]{1,0:T(8,128)(2,1)}, u32[]{:S(2)}, u32[]{:S(2)}) collective-permute-start(bf16[256,768]{1,0:T(8,128)(2,1)S(1)} %collective-permute-done.2), channel_id=1, source_target_pairs={{0,2},{2,4},{4,6},{6,8},{8,10},{10,12},{12,14},{14,16},{16,18},{18... | collective-permute-start | bytes 1179656 | tf_op jit(solution)/shard_map/ppermute | solution.py:25
  92.8 28.0 %collective-permute-start.10 = (bf16[256,768]{1,0:T(8,128)(2,1)S(1)}, bf16[256,768]{1,0:T(8,128)(2,1)S(1)}, u32[]{:S(2)}, u32[]{:S(2)}) collective-permute-start(bf16[256,768]{1,0:T(8,128)(2,1)S(1)} %collective-permute-done.9), channel_id=1, source_target_pairs={{2,0},{4,2},{6,4},{8,6},{10,8},{12,10},{14,12},{16,14},{18,16},{20... | collective-permute-start | bytes 1179656 | tf_op jit(solution)/shard_map/ppermute | solution.py:27
  104.7 18.1 %collective-permute-start.4 = (bf16[256,768]{1,0:T(8,128)(2,1)}, bf16[256,768]{1,0:T(8,128)(2,1)}, u32[]{:S(2)}, u32[]{:S(2)}) collective-permute-start(bf16[256,768]{1,0:T(8,128)(2,1)} %collective-permute-done.3), channel_id=1, source_target_pairs={{0,2},{2,4},{4,6},{6,8},{8,10},{10,12},{12,14},{14,16},{16,18},{18... | collective-permute-start | bytes 1179656 | tf_op jit(solution)/shard_map/ppermute | solution.py:25
  107.3 473.1 %reduce-scatter.14.cloned.1.call-start = ((), (), s32[]{:S(2)}) async-start(), calls=%async_computation.14 | async-start | bytes 13369344 | tf_op jit(solution)/shard_map/reduce_scatter | solution.py:215
  120.9 22.5 %collective-permute-start.11 = (bf16[256,768]{1,0:T(8,128)(2,1)S(1)}, bf16[256,768]{1,0:T(8,128)(2,1)}, u32[]{:S(2)}, u32[]{:S(2)}) collective-permute-start(bf16[256,768]{1,0:T(8,128)(2,1)S(1)} %collective-permute-done.10), channel_id=1, source_target_pairs={{2,0},{4,2},{6,4},{8,6},{10,8},{12,10},{14,12},{16,14},{18,16},{20... | collective-permute-start | bytes 1179656 | tf_op jit(solution)/shard_map/ppermute | solution.py:27
  122.8 20.6 %collective-permute-start.5 = (bf16[256,768]{1,0:T(8,128)(2,1)}, bf16[256,768]{1,0:T(8,128)(2,1)}, u32[]{:S(2)}, u32[]{:S(2)}) collective-permute-start(bf16[256,768]{1,0:T(8,128)(2,1)} %collective-permute-done.4), channel_id=1, source_target_pairs={{0,2},{2,4},{4,6},{6,8},{8,10},{10,12},{12,14},{14,16},{16,18},{18... | collective-permute-start | bytes 1179656 | tf_op jit(solution)/shard_map/ppermute | solution.py:25
  143.4 12.2 %collective-permute-start.12 = (bf16[256,768]{1,0:T(8,128)(2,1)}, bf16[256,768]{1,0:T(8,128)(2,1)}, u32[]{:S(2)}, u32[]{:S(2)}) collective-permute-start(bf16[256,768]{1,0:T(8,128)(2,1)} %collective-permute-done.11), channel_id=1, source_target_pairs={{2,0},{4,2},{6,4},{8,6},{10,8},{12,10},{14,12},{16,14},{18,16},{20... | collective-permute-start | bytes 1179656 | tf_op jit(solution)/shard_map/ppermute | solution.py:27
  143.4 12.2 %collective-permute-start.6 = (bf16[256,768]{1,0:T(8,128)(2,1)}, bf16[256,768]{1,0:T(8,128)(2,1)}, u32[]{:S(2)}, u32[]{:S(2)}) collective-permute-start(bf16[256,768]{1,0:T(8,128)(2,1)} %collective-permute-done.5), channel_id=1, source_target_pairs={{0,2},{2,4},{4,6},{6,8},{8,10},{10,12},{12,14},{14,16},{16,18},{18... | collective-permute-start | bytes 1179656 | tf_op jit(solution)/shard_map/ppermute | solution.py:25
  155.6 9.8 collective-permute-start.13
  155.6 10.0 collective-permute-start.7
  165.4 19.8 %collective-permute-start.14 = (bf16[256,768]{1,0:T(8,128)(2,1)}, bf16[256,768]{1,0:T(8,128)(2,1)S(1)}, u32[]{:S(2)}, u32[]{:S(2)}) collective-permute-start(bf16[256,768]{1,0:T(8,128)(2,1)} %collective-permute-done.13), channel_id=1, source_target_pairs={{2,0},{4,2},{6,4},{8,6},{10,8},{12,10},{14,12},{16,14},{18,16},{20... | collective-permute-start | bytes 1179656 | tf_op jit(solution)/shard_map/ppermute | solution.py:27
  446.4 158.5 %reduce-scatter.22.cloned.1.call-start = ((), (), s32[]{:S(2)}) async-start(), calls=%async_computation.18 | async-start | bytes 1769472
  474.0 154.9 %reduce-scatter.16.cloned.1.call-start = ((), (), s32[]{:S(2)}) async-start(), calls=%async_computation.15 | async-start | bytes 1769472 | tf_op jit(solution)/shard_map/reduce_scatter | solution.py:248
  475.5 216.2 %reduce-scatter.18.cloned.1.call-start = ((), (), s32[]{:S(2)}) async-start(), calls=%async_computation.16 | async-start | bytes 7077888 | tf_op jit(solution)/shard_map/reduce_scatter | solution.py:260
  480.8 273.8 %reduce-scatter.20.cloned.1.call-start = ((), (), s32[]{:S(2)}) async-start(), calls=%async_computation.17 | async-start | bytes 7077888 | tf_op jit(solution)/shard_map/reduce_scatter | solution.py:266
  486.5 292.7 %reduce-scatter.24.cloned.1.call-start = ((), (), s32[]{:S(2)}) async-start(), calls=%async_computation.19 | async-start | bytes 1769472
  583.4 220.4 %reduce-scatter.26.cloned.1.call-start = ((), (), s32[]{:S(2)}) async-start(), calls=%async_computation.20 | async-start | bytes 1769472
  585.0 178.1 %copy-start.69 = (bf16[768,768]{1,0:T(8,128)(2,1)S(1)}, bf16[768,768]{1,0:T(8,128)(2,1)}, u32[]{:S(2)}) copy-start(bf16[768,768]{1,0:T(8,128)(2,1)} %all-gather.19.cloned.1.call-done) | copy-start | bytes 3538948
  (104 other events, 1323.9 us)
Sparse Core Ops, SparseCore 0:
  9.6 24.8 all-gather.20
  36.0 22.7 all-gather.18
  60.4 22.7 all-gather.16
  85.9 82.2 all-gather.22
  169.6 23.6 all-gather.24
  194.7 62.6 all-gather.26
  258.9 62.7 all-gather.28
  446.5 133.8 reduce-scatter.13
  583.2 21.6 reduce-scatter.21
  607.1 21.7 reduce-scatter.15
  631.8 59.9 reduce-scatter.17
  694.6 59.9 reduce-scatter.19
  757.5 21.7 reduce-scatter.23
  782.0 21.7 reduce-scatter.25
